TPU v7x, 32 devices: a whole 2x2x4 slice. The times are simulated.
32 devices in a mesh: row: 8 (over y, x, core), col: 4 (over z).
Axes of the slice: x: 2, y: 2, z: 4, core: 2. Of those that a mesh axis runs over, the one named last changes fastest.
Arguments:
- stored_blocks: bfloat16 [8, 4, 64, 128, 128], P('row', 'col'), may hold values from -1 to 1
- stored_ids: int32 [8, 4, 3, 64], P('row', 'col'), may hold values from 0 to 127, as said below
- slab_blocks: bfloat16 [8, 4, 32, 128, 128], P('row', 'col'), may hold values from -1 to 1
- slab_ids: int32 [8, 4, 3, 32], P('row', 'col'), may hold values from 0 to 127, as said below
- pair_lists: int32 [8, 4, 4, 3, 256], P('row', 'col'), may hold values from 0 to 127, as said below
Outputs:
- product: bfloat16 [16384, 1024], P('row', 'col')
Inputs may be any that keep to these rules, and one draw needn't show every extreme that they name: `stored_ids`: present slots of cell (r, c) hold blocks of the panel pair made of panels r and r xor c: row index in the lower of the two panels (panel p covers block rows p * 16 to (p + 1) * 16 - 1), column index in the higher, row <= column. Every stored block lies in exactly one slot over all cells. Flags are 0 or 1; a half has at most 64 present slots and some halves have exactly 64. `slab_ids`: the slots of cell (r, c) name each block of panel r xor c and slab columns c * 2 to (c + 1) * 2 - 1 exactly once; flags are 0 or 1, and some cells have all flags 1. pair_lists[r, c, s] names, with flag 1 and ahead of every entry with flag 0, each pair of a present entry of A_s and a present entry of B_s whose column index and row index agree, once each; some list has all 256 flags 1.
All inputs are finite; a program needn't handle non-finite values.
Results may differ from a plain program's by a relative error of at most 0.001.
Values may be sent and summed in bfloat16 or wider, within the bound.
A program may use at most 128 MiB of HBM per device.

v0:
```python
import functools

import jax
import jax.numpy as jnp
from jax import lax
from jax.experimental import pallas as pl
from jax.experimental.pallas import tpu as pltpu
from jax.sharding import PartitionSpec as P

PANEL = 16
SLAB = 2
STEPS = 4
CHUNKS = 4
MESH = pl.DeviceIdType.MESH


def flipped(value, mask, bits):
    out = value
    for b in range(bits):
        w = 2**b
        out = out + ((mask // w) % 2) * (w - 2 * w * ((value // w) % 2))
    return out


def gather_kernel(
    stride, bits, own, slab, ids, out, blocks, slabs, row_ids, pair_ids, slab_ids,
    stage, dense, right_all, acc, table, scalars,
    z_send, z_recv, p_send, p_recv, b_send, b_recv, l_sem, t_sem,
):
    r = lax.axis_index("row")
    c = lax.axis_index("col")
    pos = c // stride
    rem = c % stride
    left = c - stride
    right = c + stride
    slots, edge = own.shape[0], own.shape[1]
    size = slots // CHUNKS
    slab_slots = slab.shape[0]

    def partner(s):
        return flipped(r, s * stride + rem, bits)

    def shifted(t):
        return flipped(r, t * stride, bits)

    bar = pltpu.get_barrier_semaphore()

    def greet(row, col):
        pl.semaphore_signal(bar, inc=1, device_id=(row, col), device_id_type=MESH)

    def cond_kind(s):
        return s * stride + rem > 0

    @pl.when(pos > 0)
    def _():
        greet(r, left)

    @pl.when(pos < STEPS - 1)
    def _():
        greet(r, right)

    for s in range(STEPS):
        @pl.when(cond_kind(s))
        def _():
            greet(partner(s), c)
    for t in range(1, STEPS):
        greet(shifted(t), c)

    ends = jnp.minimum(pos, 1) + jnp.minimum(STEPS - 1 - pos, 1)
    pl.semaphore_wait(bar, ends + jnp.minimum(rem, 1) + 2 * (STEPS - 1))

    def piece(ref, id_ref, ch):
        return id_ref if ch == 0 else ref.at[pl.ds((ch - 1) * size, size)]

    def landed(s, ch):
        return row_ids.at[s] if ch == 0 else blocks.at[s, pl.ds(1 + (ch - 1) * size, size)]

    def paired(s, ch):
        return pair_ids.at[s] if ch == 0 else blocks.at[s, pl.ds(1 + slots + (ch - 1) * size, size)]

    def along(src, s, ch, way):
        return pltpu.make_async_remote_copy(
            src_ref=src, dst_ref=landed(s, ch), send_sem=z_send.at[way, s, ch],
            recv_sem=z_recv.at[s, ch], device_id=(r, right if way else left), device_id_type=MESH)

    def across(src, s, ch):
        return pltpu.make_async_remote_copy(
            src_ref=src, dst_ref=paired(s, ch), send_sem=p_send.at[s, ch],
            recv_sem=p_recv.at[s, ch], device_id=(partner(s), c), device_id_type=MESH)

    def slab_copy(src, t, to, what):
        dst = slab_ids.at[t] if what == 0 else slabs.at[t, pl.ds(1, slab_slots)]
        return pltpu.make_async_remote_copy(
            src_ref=src, dst_ref=dst, send_sem=b_send.at[t, what],
            recv_sem=b_recv.at[t, what], device_id=(shifted(to), c), device_id_type=MESH)

    pieces = range(CHUNKS + 1)
    kept = 1 + CHUNKS // 2
    for ch in pieces:
        mine = piece(own, ids, ch)

        @pl.when(pos > (1 if ch >= kept else 0))
        def _():
            along(mine, pos, ch, 0).start()

        @pl.when(pos < STEPS - 1)
        def _():
            along(mine, pos, ch, 1).start()

        @pl.when(cond_kind(pos))
        def _():
            across(mine, pos, ch).start()
        if ch == 0:
            for what, src in ((0, ids), (1, slab)):
                slab_copy(src, 2, 2, what).start()
                slab_copy(src, 1, 1, what).start()
    local = (
        pltpu.make_async_copy(own, blocks.at[pos, pl.ds(1, slots)], l_sem.at[0]),
        pltpu.make_async_copy(ids, row_ids.at[pos], l_sem.at[1]),
        pltpu.make_async_copy(slab, slabs.at[0, pl.ds(1, slab_slots)], l_sem.at[2]),
        pltpu.make_async_copy(ids, slab_ids.at[0], l_sem.at[3]),
    )
    for copy in local:
        copy.start()

    zero_block = jnp.zeros((edge, edge), blocks.dtype)
    stage[0] = zero_block
    for s in range(STEPS):
        slabs[s, 0] = zero_block
    acc[...] = jnp.zeros_like(acc)
    sub = lax.broadcasted_iota(jnp.int32, (PANEL, 128), 0)
    lane = lax.broadcasted_iota(jnp.int32, (PANEL, 128), 1)

    def inverted(at_row, at_col, present, base, rows):
        value = jnp.where(present, lane[:1] + (1 + base), 0)
        hit = jnp.where(at_col == sub, value, 0)
        found = jnp.zeros((PANEL, 128), jnp.int32)
        for a in range(rows):
            most = jnp.max(jnp.where(at_row == a, hit, 0), axis=1, keepdims=True)
            found = jnp.where(lane == a, most, found)
        return found

    def process(s):
        q = partner(s)
        low, high = jnp.minimum(r, q) * PANEL, jnp.maximum(r, q) * PANEL
        t = flipped(s, pos, 2)

        def part(ref, base, turn):
            i, j = ref[s, 0:1] - low, ref[s, 1:2] - high
            keep = ref[s, 2:3] > 0
            return inverted(j if turn else i, i if turn else j, keep, base, PANEL)

        @pl.when(r < q)
        def _():
            table[0:PANEL] = jnp.maximum(part(row_ids, 0, False), part(pair_ids, slots, False))

        @pl.when(r > q)
        def _():
            table[0:PANEL] = jnp.maximum(part(row_ids, 0, True), part(pair_ids, slots, True))

        @pl.when(r == q)
        def _():
            i, j = row_ids[s, 0:1] - low, row_ids[s, 1:2] - high
            keep = row_ids[s, 2:3] > 0
            off = jnp.logical_and(keep, i != j)
            table[0:PANEL] = jnp.maximum(
                inverted(i, j, keep, 0, PANEL), inverted(j, i, off, slots, PANEL))

        table[PANEL:] = inverted(
            slab_ids[t, 4:5] - c * SLAB, slab_ids[t, 3:4] - q * PANEL, slab_ids[t, 5:6] > 0, 0, SLAB)
        fetch = pltpu.make_async_copy(table, scalars, t_sem.at[0])
        fetch.start()
        fetch.wait()

        def slab_row(k, carry):
            for n in range(SLAB):
                right_all[k, :, n * edge : (n + 1) * edge] = slabs[t, scalars[PANEL + k, n]]
            return carry

        lax.fori_loop(0, PANEL, slab_row, 0)

        def hold(to, of, count, turn):
            def some(g, carry):
                for x in range(4):
                    block = blocks[s, of + g * 4 + x]
                    stage[to + g * 4 + x] = block.T if turn else block
                return carry

            lax.fori_loop(0, count // 4, some, 0)

        @pl.when(r < q)
        def _():
            hold(1, 1, 2 * slots, False)

        @pl.when(r > q)
        def _():
            hold(1, 1, 2 * slots, True)

        @pl.when(r == q)
        def _():
            hold(1, 1, slots, False)
            hold(1 + slots, 1, slots, True)

        def fill(i, carry):
            for j in range(PANEL):
                dense[i, :, j * edge : (j + 1) * edge] = stage[scalars[j, i]]
            return carry

        lax.fori_loop(0, PANEL, fill, 0)
        depth = PANEL * edge
        slab_full = right_all[...].reshape(depth, SLAB * edge)
        group = 2

        def product(g, carry):
            lhs = dense[pl.ds(g * group, group)].reshape(group * edge, depth)
            at = pl.multiple_of(g * group * edge, group * edge)
            acc[pl.ds(at, group * edge)] += jnp.dot(
                lhs, slab_full, preferred_element_type=jnp.float32)
            return carry

        lax.fori_loop(0, PANEL // group, product, 0)

    second = jnp.where(pos == 2, 1, 2)
    last = jnp.where(pos == 0, 1, jnp.where(pos == 1, 3, 0))
    third = 6 - pos - second - last

    def take(s):
        for ch in pieces:
            @pl.when(cond_kind(s))
            def _():
                across(landed(s, ch), s, ch).wait_recv()
        process(s)

    for d in range(1, STEPS):
        for ch in pieces:
            for way in (1, 0):
                s = pos - d if way else pos + d
                here = s >= 0 if way else s <= STEPS - 1
                if d == 1 and not way and ch >= kept:
                    here = jnp.logical_and(here, pos > 0)
                more = pos < STEPS - 1 if way else pos > 0

                @pl.when(here)
                def _():
                    along(landed(s, ch), s, ch, way).wait_recv()

                    @pl.when(more)
                    def _():
                        along(landed(s, ch), s, ch, way).start()

                    @pl.when(cond_kind(s))
                    def _():
                        across(landed(s, ch), s, ch).start()
            if d == 1 and ch == 1:
                for what, src in ((0, slab_ids.at[2]), (1, slabs.at[2, pl.ds(1, slab_slots)])):
                    slab_copy(src, 2, 2, what).wait_recv()
                    slab_copy(src, 3, 1, what).start()

        if d == 1:
            for copy in local:
                copy.wait()
            for what, src in ((0, ids), (1, slab)):
                slab_copy(src, 1, 1, what).wait()
                slab_copy(src, 2, 2, what).wait_send()
                slab_copy(src, 3, 1, what).wait()
            take(pos)
        if d == 2:
            @pl.when(pos == 1)
            def _():
                for ch in range(kept, CHUNKS + 1):
                    along(piece(own, ids, ch), pos, ch, 0).start()

            take(second)
    take(third)

    @pl.when(pos == 0)
    def _():
        for ch in range(kept, CHUNKS + 1):
            along(landed(1, ch), 1, ch, 0).wait_recv()
            across(landed(1, ch), 1, ch).start()

    take(last)
    out[...] = acc[...].astype(out.dtype)
    for s in range(STEPS):
        for ch in pieces:
            @pl.when(cond_kind(s))
            def _():
                across(landed(s, ch), s, ch).wait_send()

            @pl.when(jnp.logical_and(s <= pos, pos < STEPS - 1))
            def _():
                along(landed(s, ch), s, ch, 1).wait_send()

            @pl.when(jnp.logical_and(s >= pos, pos > 0))
            def _():
                along(landed(s, ch), s, ch, 0).wait_send()


def gather(own, slab, ids, stride, bits):
    any_spec = pl.BlockSpec(memory_space=pl.ANY)
    dma = pltpu.SemaphoreType.DMA
    slots, edge = own.shape[0], own.shape[1]
    tile = (PANEL * edge, SLAB * edge)
    listed = pltpu.VMEM((STEPS,) + ids.shape, ids.dtype)
    return pl.pallas_call(
        functools.partial(gather_kernel, stride, bits),
        out_shape=jax.ShapeDtypeStruct(tile, own.dtype),
        in_specs=[any_spec] * 3,
        out_specs=pl.BlockSpec(memory_space=pltpu.VMEM),
        scratch_shapes=[
            pltpu.VMEM((STEPS, 2 * slots + 1, edge, edge), own.dtype),
            pltpu.VMEM((STEPS, slab.shape[0] + 1, edge, edge), own.dtype),
            listed, listed, listed,
            pltpu.VMEM((2 * slots + 1, edge, edge), own.dtype),
            pltpu.VMEM((PANEL, edge, PANEL * edge), own.dtype),
            pltpu.VMEM((PANEL, edge, SLAB * edge), own.dtype),
            pltpu.VMEM(tile, jnp.float32),
            pltpu.VMEM((2 * PANEL, 128), jnp.int32),
            pltpu.SMEM((2 * PANEL, 128), jnp.int32),
            dma((2, STEPS, CHUNKS + 1)), dma((STEPS, CHUNKS + 1)),
            dma((STEPS, CHUNKS + 1)), dma((STEPS, CHUNKS + 1)),
            dma((STEPS, 2)), dma((STEPS, 2)), dma((4,)), dma((1,)),
        ],
        compiler_params=pltpu.CompilerParams(
            collective_id=0, has_side_effects=True, vmem_limit_bytes=56 * 2**20
        ),
    )(own, slab, ids)


def on_device(stored_blocks, stored_ids, slab_blocks, slab_ids, pair_lists):
    stride = lax.axis_size("col") // STEPS
    bits = lax.axis_size("row").bit_length() - 1
    ids = jnp.concatenate(
        [
            jnp.pad(stored_ids[0, 0], ((0, 0), (0, 128 - stored_ids.shape[-1]))),
            jnp.pad(slab_ids[0, 0], ((0, 2), (0, 128 - slab_ids.shape[-1]))),
        ]
    )
    return gather(stored_blocks[0, 0], slab_blocks[0, 0], ids, stride, bits)


def solution(mesh):
    return jax.shard_map(
        on_device,
        mesh=mesh,
        in_specs=(
            P("row", "col", None, None, None),
            P("row", "col", None, None),
            P("row", "col", None, None, None),
            P("row", "col", None, None),
            P("row", "col", None, None, None),
        ),
        out_specs=P("row", "col"),
        check_vma=False,
    )
```

profile of v0, /device:TPU:25, one launch (start us, length us, event | category | flops | bytes accessed | tf_op | source)
XLA Modules:
  0.0 163.7 jit_solution(14234175956978626109)
XLA Ops:
  0.0 0.7 copy.10
  0.7 0.7 copy.9
  1.4 0.6 pad_add_fusion.ids
  2.0 159.4 %shard_map.46 = bf16[2048,256]{1,0:T(8,128)(2,1)} custom-call(bf16[64,128,128]{2,1,0:T(8,128)(2,1)} %bitcast.8, bf16[32,128,128]{2,1,0:T(8,128)(2,1)} %bitcast.9, s32[8,128]{1,0:T(8,128)} %pad_add_fusion.ids), custom_call_target="tpu_custom_call" | custom-call | tf_op jit(solution)/shard_map/pallas_call | solution.py:305
  161.4 2.3 %copy.12 = bf16[2048,256]{1,0:T(8,128)(2,1)} copy(bf16[2048,256]{1,0:T(8,128)(2,1)} %shard_map.46) | data formatting | bytes 2097152
where the time goes:
time: 167 us; the launch traced here: 164 us
  Pallas kernels  159 us (95%)
  local copies, waits for them, and re-layouts  3.62 us (2%)
    pallas_call x1, Pallas kernels, gather(): pl.pallas_call(functools.partial(gather_kernel, stride, bits), out_shape=...  159 us
    unnamed x3, local copies, waits for them, and re-layouts  3.62 us

commit v1 on v0

--- a/solution.py
+++ b/solution.py
@@ -10,7 +10,7 @@
 PANEL = 16
 SLAB = 2
 STEPS = 4
-CHUNKS = 4
+CHUNKS = 8
 MESH = pl.DeviceIdType.MESH
 
 
@@ -23,8 +23,8 @@
 
 
 def gather_kernel(
-    stride, bits, own, slab, ids, out, blocks, slabs, row_ids, pair_ids, slab_ids,
-    stage, dense, right_all, acc, table, scalars,
+    stride, bits, own, slab, ids, names, out, blocks, slabs, row_ids, pair_ids, slab_ids,
+    stage, right_all, acc, table, scalars,
     z_send, z_recv, p_send, p_recv, b_send, b_recv, l_sem, t_sem,
 ):
     r = lax.axis_index("row")
@@ -111,28 +111,29 @@
         def _():
             across(mine, pos, ch).start()
         if ch == 0:
-            for what, src in ((0, ids), (1, slab)):
+            for what, src in ((0, names), (1, slab)):
                 slab_copy(src, 2, 2, what).start()
                 slab_copy(src, 1, 1, what).start()
     local = (
         pltpu.make_async_copy(own, blocks.at[pos, pl.ds(1, slots)], l_sem.at[0]),
         pltpu.make_async_copy(ids, row_ids.at[pos], l_sem.at[1]),
         pltpu.make_async_copy(slab, slabs.at[0, pl.ds(1, slab_slots)], l_sem.at[2]),
-        pltpu.make_async_copy(ids, slab_ids.at[0], l_sem.at[3]),
+        pltpu.make_async_copy(names, slab_ids.at[0], l_sem.at[3]),
     )
     for copy in local:
         copy.start()
 
     zero_block = jnp.zeros((edge, edge), blocks.dtype)
-    stage[0] = zero_block
     for s in range(STEPS):
         slabs[s, 0] = zero_block
-    acc[...] = jnp.zeros_like(acc)
-    sub = lax.broadcasted_iota(jnp.int32, (PANEL, 128), 0)
-    lane = lax.broadcasted_iota(jnp.int32, (PANEL, 128), 1)
+        stage[s, 0] = zero_block
 
     def inverted(at_row, at_col, present, base, rows):
-        value = jnp.where(present, lane[:1] + (1 + base), 0)
+        count = at_row.shape[1]
+        sub = lax.broadcasted_iota(jnp.int32, (PANEL, count), 0)
+        first = lax.broadcasted_iota(jnp.int32, (1, count), 1)
+        lane = lax.broadcasted_iota(jnp.int32, (PANEL, 128), 1)
+        value = jnp.where(present, first + (1 + base), 0)
         hit = jnp.where(at_col == sub, value, 0)
         found = jnp.zeros((PANEL, 128), jnp.int32)
         for a in range(rows):
@@ -140,14 +141,14 @@
             found = jnp.where(lane == a, most, found)
         return found
 
-    def process(s):
+    def prepare(s):
         q = partner(s)
         low, high = jnp.minimum(r, q) * PANEL, jnp.maximum(r, q) * PANEL
         t = flipped(s, pos, 2)
 
         def part(ref, base, turn):
-            i, j = ref[s, 0:1] - low, ref[s, 1:2] - high
-            keep = ref[s, 2:3] > 0
+            i, j = ref[s, 0] - low, ref[s, 1] - high
+            keep = ref[s, 2] > 0
             return inverted(j if turn else i, i if turn else j, keep, base, PANEL)
 
         @pl.when(r < q)
@@ -160,62 +161,79 @@
 
         @pl.when(r == q)
         def _():
-            i, j = row_ids[s, 0:1] - low, row_ids[s, 1:2] - high
-            keep = row_ids[s, 2:3] > 0
+            i, j = row_ids[s, 0] - low, row_ids[s, 1] - high
+            keep = row_ids[s, 2] > 0
             off = jnp.logical_and(keep, i != j)
             table[0:PANEL] = jnp.maximum(
                 inverted(i, j, keep, 0, PANEL), inverted(j, i, off, slots, PANEL))
 
         table[PANEL:] = inverted(
-            slab_ids[t, 4:5] - c * SLAB, slab_ids[t, 3:4] - q * PANEL, slab_ids[t, 5:6] > 0, 0, SLAB)
-        fetch = pltpu.make_async_copy(table, scalars, t_sem.at[0])
+            slab_ids[t, 1] - c * SLAB, slab_ids[t, 0] - q * PANEL, slab_ids[t, 2] > 0, 0, SLAB)
+        fetch = pltpu.make_async_copy(table, scalars.at[s], t_sem.at[0])
         fetch.start()
         fetch.wait()
 
         def slab_row(k, carry):
             for n in range(SLAB):
-                right_all[k, :, n * edge : (n + 1) * edge] = slabs[t, scalars[PANEL + k, n]]
+                right_all[s, k, :, n * edge : (n + 1) * edge] = slabs[t, scalars[s, PANEL + k, n]]
             return carry
 
         lax.fori_loop(0, PANEL, slab_row, 0)
 
-        def hold(to, of, count, turn):
-            def some(g, carry):
-                for x in range(4):
-                    block = blocks[s, of + g * 4 + x]
-                    stage[to + g * 4 + x] = block.T if turn else block
-                return carry
-
-            lax.fori_loop(0, count // 4, some, 0)
-
-        @pl.when(r < q)
-        def _():
-            hold(1, 1, 2 * slots, False)
-
-        @pl.when(r > q)
-        def _():
-            hold(1, 1, 2 * slots, True)
-
-        @pl.when(r == q)
-        def _():
-            hold(1, 1, slots, False)
-            hold(1 + slots, 1, slots, True)
-
-        def fill(i, carry):
-            for j in range(PANEL):
-                dense[i, :, j * edge : (j + 1) * edge] = stage[scalars[j, i]]
+    def move(s, to, of, turn):
+        def some(g, carry):
+            for x in range(4):
+                block = blocks[s, of + g * 4 + x]
+                stage[s, to + g * 4 + x] = block.T if turn else block
             return carry
 
-        lax.fori_loop(0, PANEL, fill, 0)
-        depth = PANEL * edge
-        slab_full = right_all[...].reshape(depth, SLAB * edge)
-        group = 2
+        lax.fori_loop(0, size // 4, some, 0)
+
+    def hold(s, at):
+        turned = r > partner(s)
+
+        @pl.when(turned)
+        def _():
+            move(s, at, at, True)
+
+        @pl.when(jnp.logical_not(turned))
+        def _():
+            move(s, at, at, False)
+
+    def hold_row(s, ch):
+        at = 1 + (ch - 1) * size
+        hold(s, at)
+
+        @pl.when(jnp.logical_not(cond_kind(s)))
+        def _():
+            move(s, slots + at, at, True)
+
+    def hold_pair(s, ch):
+        @pl.when(cond_kind(s))
+        def _():
+            hold(s, 1 + slots + (ch - 1) * size)
+
+    depth = PANEL * edge
+    group = 4
+
+    def multiply(s, first, final):
+        slab_full = right_all[s].reshape(depth, SLAB * edge)
 
         def product(g, carry):
-            lhs = dense[pl.ds(g * group, group)].reshape(group * edge, depth)
+            rows = []
+            for a in range(group):
+                i = g * group + a
+                rows.append(jnp.concatenate(
+                    [stage[s, scalars[s, j, i]] for j in range(PANEL)], axis=1))
             at = pl.multiple_of(g * group * edge, group * edge)
-            acc[pl.ds(at, group * edge)] += jnp.dot(
-                lhs, slab_full, preferred_element_type=jnp.float32)
+            total = jnp.dot(
+                jnp.concatenate(rows, axis=0), slab_full, preferred_element_type=jnp.float32)
+            if not first:
+                total = total + acc[pl.ds(at, group * edge)]
+            if final:
+                out[pl.ds(at, group * edge)] = total.astype(out.dtype)
+            else:
+                acc[pl.ds(at, group * edge)] = total
             return carry
 
         lax.fori_loop(0, PANEL // group, product, 0)
@@ -224,12 +242,19 @@
     last = jnp.where(pos == 0, 1, jnp.where(pos == 1, 3, 0))
     third = 6 - pos - second - last
 
-    def take(s):
-        for ch in pieces:
-            @pl.when(cond_kind(s))
-            def _():
-                across(landed(s, ch), s, ch).wait_recv()
-        process(s)
+    def crossed(s, ch):
+        @pl.when(cond_kind(s))
+        def _():
+            across(landed(s, ch), s, ch).wait_recv()
+
+    def take(s, first=False):
+        crossed(s, 0)
+        prepare(s)
+        for ch in range(1, CHUNKS + 1):
+            hold_row(s, ch)
+            crossed(s, ch)
+            hold_pair(s, ch)
+        multiply(s, first, False)
 
     for d in range(1, STEPS):
         for ch in pieces:
@@ -259,11 +284,11 @@
         if d == 1:
             for copy in local:
                 copy.wait()
-            for what, src in ((0, ids), (1, slab)):
+            for what, src in ((0, names), (1, slab)):
                 slab_copy(src, 1, 1, what).wait()
                 slab_copy(src, 2, 2, what).wait_send()
                 slab_copy(src, 3, 1, what).wait()
-            take(pos)
+            take(pos, True)
         if d == 2:
             @pl.when(pos == 1)
             def _():
@@ -273,14 +298,19 @@
             take(second)
     take(third)
 
-    @pl.when(pos == 0)
-    def _():
-        for ch in range(kept, CHUNKS + 1):
-            along(landed(1, ch), 1, ch, 0).wait_recv()
-            across(landed(1, ch), 1, ch).start()
-
-    take(last)
-    out[...] = acc[...].astype(out.dtype)
+    crossed(last, 0)
+    prepare(last)
+    for ch in range(1, CHUNKS + 1):
+        if ch >= kept:
+            @pl.when(pos == 0)
+            def _():
+                along(landed(1, ch), 1, ch, 0).wait_recv()
+                across(landed(1, ch), 1, ch).start()
+
+        hold_row(last, ch)
+        crossed(last, ch)
+        hold_pair(last, ch)
+    multiply(last, False, True)
     for s in range(STEPS):
         for ch in pieces:
             @pl.when(cond_kind(s))
@@ -296,7 +326,7 @@
                 along(landed(s, ch), s, ch, 0).wait_send()
 
 
-def gather(own, slab, ids, stride, bits):
+def gather(own, slab, ids, names, stride, bits):
     any_spec = pl.BlockSpec(memory_space=pl.ANY)
     dma = pltpu.SemaphoreType.DMA
     slots, edge = own.shape[0], own.shape[1]
@@ -305,18 +335,17 @@
     return pl.pallas_call(
         functools.partial(gather_kernel, stride, bits),
         out_shape=jax.ShapeDtypeStruct(tile, own.dtype),
-        in_specs=[any_spec] * 3,
+        in_specs=[any_spec] * 4,
         out_specs=pl.BlockSpec(memory_space=pltpu.VMEM),
         scratch_shapes=[
             pltpu.VMEM((STEPS, 2 * slots + 1, edge, edge), own.dtype),
             pltpu.VMEM((STEPS, slab.shape[0] + 1, edge, edge), own.dtype),
-            listed, listed, listed,
-            pltpu.VMEM((2 * slots + 1, edge, edge), own.dtype),
-            pltpu.VMEM((PANEL, edge, PANEL * edge), own.dtype),
-            pltpu.VMEM((PANEL, edge, SLAB * edge), own.dtype),
+            listed, listed, pltpu.VMEM((STEPS,) + names.shape, names.dtype),
+            pltpu.VMEM((STEPS, 2 * slots + 1, edge, edge), own.dtype),
+            pltpu.VMEM((STEPS, PANEL, edge, SLAB * edge), own.dtype),
             pltpu.VMEM(tile, jnp.float32),
             pltpu.VMEM((2 * PANEL, 128), jnp.int32),
-            pltpu.SMEM((2 * PANEL, 128), jnp.int32),
+            pltpu.SMEM((STEPS, 2 * PANEL, 128), jnp.int32),
             dma((2, STEPS, CHUNKS + 1)), dma((STEPS, CHUNKS + 1)),
             dma((STEPS, CHUNKS + 1)), dma((STEPS, CHUNKS + 1)),
             dma((STEPS, 2)), dma((STEPS, 2)), dma((4,)), dma((1,)),
@@ -324,19 +353,15 @@
         compiler_params=pltpu.CompilerParams(
             collective_id=0, has_side_effects=True, vmem_limit_bytes=56 * 2**20
         ),
-    )(own, slab, ids)
+    )(own, slab, ids, names)
 
 
 def on_device(stored_blocks, stored_ids, slab_blocks, slab_ids, pair_lists):
     stride = lax.axis_size("col") // STEPS
     bits = lax.axis_size("row").bit_length() - 1
-    ids = jnp.concatenate(
-        [
-            jnp.pad(stored_ids[0, 0], ((0, 0), (0, 128 - stored_ids.shape[-1]))),
-            jnp.pad(slab_ids[0, 0], ((0, 2), (0, 128 - slab_ids.shape[-1]))),
-        ]
-    )
-    return gather(stored_blocks[0, 0], slab_blocks[0, 0], ids, stride, bits)
+    ids = stored_ids.reshape(stored_ids.shape[2], 1, stored_ids.shape[3])
+    names = slab_ids.reshape(slab_ids.shape[2], 1, slab_ids.shape[3])
+    return gather(stored_blocks[0, 0], slab_blocks[0, 0], ids, names, stride, bits)
 
 
 def solution(mesh):

time: 167 us -> 157 us (0.940); the launches traced: 164 us -> 157 us
  Pallas kernels: 159 us -> 154 us
    pallas_call x1, Pallas kernels: 159 us -> 154 us  [gather(): pl.pallas_call(functools.partial(gather_kernel, stride, bits), out_shape=...]
    unnamed x3 -> x1, local copies, waits for them, and re-layouts: 3.62 us -> 2.26 us
where the time goes in v1:
time: 157 us
  Pallas kernels  154 us (98%)
  local copies, waits for them, and re-layouts  2.26 us (1%)
    pallas_call x1, Pallas kernels, gather(): pl.pallas_call(functools.partial(gather_kernel, stride, bits), out_shape=...  154 us

profile of v1, /device:TPU:25, one launch (start us, length us, event | category | flops | bytes accessed | tf_op | source)
XLA Modules:
  0.0 156.6 jit_solution(16728928062433325007)
XLA Ops:
  0.0 154.3 %shard_map.46 = bf16[2048,256]{1,0:T(8,128)(2,1)} custom-call(bf16[64,128,128]{2,1,0:T(8,128)(2,1)} %bitcast.4, bf16[32,128,128]{2,1,0:T(8,128)(2,1)} %bitcast.5, s32[3,1,64]{2,1,0:T(1,128)} %bitcast.6, s32[3,1,32]{2,1,0:T(1,128)} %bitcast.7), custom_call_target="tpu_custom_call" | custom-call | tf_op jit(solution)/shard_map/pallas_call | solution.py:335
  154.3 2.3 %copy.6 = bf16[2048,256]{1,0:T(8,128)(2,1)} copy(bf16[2048,256]{1,0:T(8,128)(2,1)} %shard_map.46) | data formatting | bytes 2097152

commit v2 on v1

v2 whole, which is shorter than its diff:
```python
import functools

import jax
import jax.numpy as jnp
from jax import lax
from jax.experimental import pallas as pl
from jax.experimental.pallas import tpu as pltpu
from jax.sharding import PartitionSpec as P

PANEL = 16
SLAB = 2
STEPS = 4
CHUNKS = 8
FORWARDED = 2
GROUPS = 4
MESH = pl.DeviceIdType.MESH


def flipped(value, mask, bits):
    out = value
    for b in range(bits):
        w = 2**b
        out = out + ((mask // w) % 2) * (w - 2 * w * ((value // w) % 2))
    return out


def product_kernel(
    stride, bits, own, slab, ids, names, out, blocks, slabs, row_ids, pair_ids, slab_ids,
    stage, right_all, acc, result, table, scalars,
    z_send, z_recv, p_send, p_recv, f_send, b_send, b_recv, o_send, o_recv, l_sem, t_sem,
):
    r = lax.axis_index("row")
    c = lax.axis_index("col")
    pos = c // stride
    rem = c % stride
    slots, edge = own.shape[0], own.shape[1]
    size = slots // CHUNKS
    slab_slots = slab.shape[0]
    width = SLAB * edge
    worker = jnp.logical_and(pos > 0, pos < STEPS - 1)
    low_side = pos < STEPS // 2
    ahead = jnp.where(low_side, c + stride, c - stride)
    behind = jnp.where(low_side, c - stride, c + stride)
    fed = jnp.where(low_side, 0, STEPS - 1)
    near = STEPS - 1 - pos
    far = STEPS - 1 - fed
    fed_col = jnp.where(worker, behind, c)

    def partner(s):
        return flipped(r, s * stride + rem, bits)

    def shifted(t):
        return flipped(r, t * stride, bits)

    bar = pltpu.get_barrier_semaphore()

    def greet(row, col):
        pl.semaphore_signal(bar, inc=1, device_id=(row, col), device_id_type=MESH)

    def cond_kind(s):
        return s * stride + rem > 0

    greet(r, ahead)
    greet(shifted(2), c)

    @pl.when(worker)
    def _():
        greet(r, behind)
        greet(shifted(1), c)
        for s in range(STEPS):
            @pl.when(cond_kind(s))
            def _():
                greet(partner(s), c)

    @pl.when(pos == STEPS - 1)
    def _():
        greet(partner(STEPS - 1), c)

    @pl.when(worker)
    def _():
        pl.semaphore_wait(bar, 4 + (STEPS - 1) + jnp.minimum(rem, 1))

    @pl.when(pos == STEPS - 1)
    def _():
        pl.semaphore_wait(bar, 3)

    @pl.when(pos == 0)
    def _():
        pl.semaphore_wait(bar, 2)

    pieces = range(CHUNKS + 1)
    tail = range(CHUNKS + 1 - FORWARDED, CHUNKS + 1)

    def span(ch):
        return pl.ds((ch - 1) * size, size)

    def mine(ch):
        return ids if ch == 0 else own.at[span(ch)]

    def landed(s, ch):
        return row_ids.at[s] if ch == 0 else blocks.at[s, span(ch)]

    def paired(s, ch):
        return pair_ids.at[s] if ch == 0 else blocks.at[s, pl.ds(slots + (ch - 1) * size, size)]

    def along(src, s, ch):
        return pltpu.make_async_remote_copy(
            src_ref=src, dst_ref=landed(s, ch), send_sem=z_send.at[s, ch],
            recv_sem=z_recv.at[s, ch], device_id=(r, ahead), device_id_type=MESH)

    def across(src, s, ch):
        return pltpu.make_async_remote_copy(
            src_ref=src, dst_ref=paired(s, ch), send_sem=p_send.at[s, ch],
            recv_sem=p_recv.at[s, ch], device_id=(partner(s), c), device_id_type=MESH)

    def forward(ch):
        return pltpu.make_async_remote_copy(
            src_ref=paired(pos, ch), dst_ref=paired(pos, ch), send_sem=f_send.at[ch],
            recv_sem=p_recv.at[pos, ch], device_id=(r, ahead), device_id_type=MESH)

    def tile(side, t, what):
        return slab_ids.at[side, t] if what == 0 else slabs.at[side, t, pl.ds(1, slab_slots)]

    def slab_copy(src, side, t, what, to):
        return pltpu.make_async_remote_copy(
            src_ref=src, dst_ref=tile(side, t, what), send_sem=b_send.at[side, t, what],
            recv_sem=b_recv.at[side, t, what], device_id=to, device_id_type=MESH)

    def give(side, t, to, srcs):
        for what in range(2):
            slab_copy(srcs[what], side, t, what, to).start()

    def have(side, t):
        for what in range(2):
            slab_copy(tile(side, t, what), side, t, what, (r, c)).wait_recv()

    def gave(side, t):
        for what in range(2):
            slab_copy(tile(side, t, what), side, t, what, (r, c)).wait_send()

    def tiles(side, t):
        return tile(side, t, 0), tile(side, t, 1)

    block_rows = PANEL // GROUPS

    def returned(g):
        at = pl.ds(pl.multiple_of(g * block_rows * edge, block_rows * edge), block_rows * edge)
        return pltpu.make_async_remote_copy(
            src_ref=result.at[at], dst_ref=result.at[at], send_sem=o_send.at[g],
            recv_sem=o_recv.at[g], device_id=(r, behind), device_id_type=MESH)

    def got(g):
        at = pl.ds(pl.multiple_of(g * block_rows * edge, block_rows * edge), block_rows * edge)
        return pltpu.make_async_remote_copy(
            src_ref=result.at[at], dst_ref=result.at[at], send_sem=o_send.at[g],
            recv_sem=o_recv.at[g], device_id=(r, ahead), device_id_type=MESH)

    plane_two = (shifted(2), c)
    plane_one = (shifted(1), c)
    inward = (r, ahead)
    give(0, 2, plane_two, (names, slab))

    @pl.when(jnp.logical_not(worker))
    def _():
        give(1, 0, inward, (names, slab))
        for ch in range(3):
            along(mine(ch), pos, ch).start()

        @pl.when(pos > 0)
        def _():
            for ch in tail:
                across(mine(ch), pos, ch).start()

        have(0, 2)
        give(1, 2, inward, tiles(0, 2))
        for ch in range(3, CHUNKS + 1):
            along(mine(ch), pos, ch).start()

        @pl.when(pos > 0)
        def _():
            for ch in tail:
                across(mine(ch), pos, ch).wait_recv()
                forward(ch).start()

        for g in range(GROUPS):
            got(g).wait_recv()
            at = pl.ds(g * block_rows * edge, block_rows * edge)
            out[at] = result[at]
        gave(0, 2)
        gave(1, 0)
        gave(1, 2)
        for ch in pieces:
            along(mine(ch), pos, ch).wait_send()

        @pl.when(pos > 0)
        def _():
            for ch in tail:
                across(mine(ch), pos, ch).wait_send()
                forward(ch).wait_send()

    def held_back(s, ch):
        return s == pos + 1 if ch in tail else False

    def send_across(src, s, ch):
        @pl.when(jnp.logical_and(cond_kind(s), jnp.logical_not(held_back(s, ch))))
        def _():
            across(src, s, ch).start()

    def crossed(s, ch):
        waits = cond_kind(s)
        if s == 2 and ch in tail:
            waits = jnp.logical_and(waits, pos != 2)

        @pl.when(waits)
        def _():
            across(landed(s, ch), s, ch).wait_recv()

    def inverted(at_row, at_col, present, base, rows):
        count = at_row.shape[1]
        sub = lax.broadcasted_iota(jnp.int32, (PANEL, count), 0)
        first = lax.broadcasted_iota(jnp.int32, (1, count), 1)
        lane = lax.broadcasted_iota(jnp.int32, (PANEL, 128), 1)
        value = jnp.where(present, first + (1 + base), 0)
        hit = jnp.where(at_col == sub, value, 0)
        found = jnp.zeros((PANEL, 128), jnp.int32)
        for a in range(rows):
            most = jnp.max(jnp.where(at_row == a, hit, 0), axis=1, keepdims=True)
            found = jnp.where(lane == a, most, found)
        return found

    def prepare(s):
        q = partner(s)
        low, high = jnp.minimum(r, q) * PANEL, jnp.maximum(r, q) * PANEL

        def part(ref, base, turn):
            i, j = ref[s, 0] - low, ref[s, 1] - high
            keep = ref[s, 2] > 0
            return inverted(j if turn else i, i if turn else j, keep, base, PANEL)

        @pl.when(r < q)
        def _():
            table[0:PANEL] = jnp.maximum(part(row_ids, 0, False), part(pair_ids, slots, False))

        @pl.when(r > q)
        def _():
            table[0:PANEL] = jnp.maximum(part(row_ids, 0, True), part(pair_ids, slots, True))

        @pl.when(r == q)
        def _():
            i, j = row_ids[s, 0] - low, row_ids[s, 1] - high
            keep = row_ids[s, 2] > 0
            off = jnp.logical_and(keep, i != j)
            table[0:PANEL] = jnp.maximum(
                inverted(i, j, keep, 0, PANEL), inverted(j, i, off, slots, PANEL))

        places = ((0, flipped(s, pos, 2), c), (1, flipped(s, fed, 2), fed_col))
        for side, t, col in places:
            table[(1 + side) * PANEL : (2 + side) * PANEL] = inverted(
                slab_ids[side, t, 1] - col * SLAB, slab_ids[side, t, 0] - q * PANEL,
                slab_ids[side, t, 2] > 0, 0, SLAB)
        fetch = pltpu.make_async_copy(table, scalars.at[s], t_sem.at[0])
        fetch.start()
        fetch.wait()

        def slab_row(k, carry):
            for side, t, _ in places:
                for n in range(SLAB):
                    at = side * width + n * edge
                    right_all[k, :, at : at + edge] = slabs[
                        side, t, scalars[s, (1 + side) * PANEL + k, n]]
            return carry

        lax.fori_loop(0, PANEL, slab_row, 0)

    def move(s, to, of, turn):
        def some(g, carry):
            for x in range(4):
                block = blocks[s, of + g * 4 + x]
                stage[1 + to + g * 4 + x] = block.T if turn else block
            return carry

        lax.fori_loop(0, size // 4, some, 0)

    def hold(s, at):
        turned = r > partner(s)

        @pl.when(turned)
        def _():
            move(s, at, at, True)

        @pl.when(jnp.logical_not(turned))
        def _():
            move(s, at, at, False)

    def hold_row(s, ch):
        at = (ch - 1) * size
        hold(s, at)

        @pl.when(jnp.logical_not(cond_kind(s)))
        def _():
            move(s, slots + at, at, True)

    def hold_pair(s, ch):
        @pl.when(cond_kind(s))
        def _():
            hold(s, slots + (ch - 1) * size)

    depth = PANEL * edge

    def rows_of(g):
        return pl.ds(pl.multiple_of(g * block_rows * edge, block_rows * edge), block_rows * edge)

    def some_rows(s, g, right):
        rows = []
        for a in range(block_rows):
            rows.append(jnp.concatenate(
                [stage[scalars[s, j, g * block_rows + a]] for j in range(PANEL)], axis=1))
        return jnp.dot(
            jnp.concatenate(rows, axis=0), right, preferred_element_type=jnp.float32)

    def multiply(s, first):
        right = right_all[...].reshape(depth, 2 * width)

        def product(g, carry):
            total = some_rows(s, g, right)
            acc[rows_of(g)] = total if first else total + acc[rows_of(g)]
            return carry

        lax.fori_loop(0, GROUPS, product, 0)

    def take(s, first=False):
        crossed(s, 0)
        prepare(s)
        for ch in range(1, CHUNKS + 1):
            hold_row(s, ch)
            crossed(s, ch)
            hold_pair(s, ch)
        multiply(s, first)

    @pl.when(worker)
    def _():
        give(0, 1, plane_one, (names, slab))
        for ch in pieces:
            along(mine(ch), pos, ch).start()
        for ch in (0, *tail, *range(1, CHUNKS + 1 - FORWARDED)):
            send_across(mine(ch), pos, ch)
        local = (
            pltpu.make_async_copy(own, blocks.at[pos, pl.ds(0, slots)], l_sem.at[0]),
            pltpu.make_async_copy(ids, row_ids.at[pos], l_sem.at[1]),
            pltpu.make_async_copy(slab, slabs.at[0, 0, pl.ds(1, slab_slots)], l_sem.at[2]),
            pltpu.make_async_copy(names, slab_ids.at[0, 0], l_sem.at[3]),
        )
        for copy in local:
            copy.start()
        zero_block = jnp.zeros((edge, edge), blocks.dtype)
        for side in range(2):
            for t in range(STEPS):
                slabs[side, t, 0] = zero_block
        stage[0] = zero_block

        def relay_fed(ch):
            along(landed(fed, ch), fed, ch).wait_recv()
            along(landed(fed, ch), fed, ch).start()
            send_across(landed(fed, ch), fed, ch)

        for ch in pieces:
            along(landed(near, ch), near, ch).wait_recv()
            send_across(landed(near, ch), near, ch)
            if ch == 2:
                have(0, 2)
                give(0, 3, plane_one, tiles(0, 2))
            if ch == 4:
                have(1, 0)
                give(1, 1, plane_one, tiles(1, 0))
            if ch == 6:
                for n in range(3):
                    relay_fed(n)

        @pl.when(pos == 2)
        def _():
            for ch in tail:
                across(landed(pos, ch), pos, ch).wait_recv()
                forward(ch).start()

        have(1, 2)
        give(1, 3, plane_one, tiles(1, 2))
        for copy in local:
            copy.wait()
        have(0, 1)
        have(0, 3)
        have(1, 1)
        have(1, 3)

        take(1, True)
        for ch in pieces:
            if ch > 2:
                relay_fed(ch)
            along(landed(far, ch), far, ch).wait_recv()
            send_across(landed(far, ch), far, ch)
            if ch == 4:
                take(2)
        take(0)
        s = STEPS - 1
        crossed(s, 0)
        prepare(s)
        for ch in range(1, CHUNKS + 1):
            hold_row(s, ch)
            crossed(s, ch)
            hold_pair(s, ch)
        right = right_all[:, :, width:].reshape(depth, width)

        def last_away(g, carry):
            total = some_rows(s, g, right) + acc[rows_of(g), width:]
            result[rows_of(g)] = total.astype(result.dtype)

            @pl.when(g > 0)
            def _():
                returned(g - 1).start()
            return carry

        lax.fori_loop(0, GROUPS, last_away, 0)
        kept = right_all[:, :, :width].reshape(depth, width)

        def last_here(g, carry):
            total = some_rows(s, g, kept) + acc[rows_of(g), :width]
            out[rows_of(g)] = total.astype(out.dtype)

            @pl.when(g == 0)
            def _():
                returned(GROUPS - 1).start()
            return carry

        lax.fori_loop(0, GROUPS, last_here, 0)
        for t in range(1, STEPS):
            gave(0, t)
        gave(1, 1)
        gave(1, 3)
        for ch in pieces:
            for s in range(STEPS):
                @pl.when(jnp.logical_and(cond_kind(s), jnp.logical_not(held_back(s, ch))))
                def _():
                    across(landed(s, ch), s, ch).wait_send()
            along(landed(pos, ch), pos, ch).wait_send()
            along(landed(fed, ch), fed, ch).wait_send()

        @pl.when(pos == 2)
        def _():
            for ch in tail:
                forward(ch).wait_send()

        for g in range(GROUPS):
            returned(g).wait_send()


def product_call(own, slab, ids, names, stride, bits):
    any_spec = pl.BlockSpec(memory_space=pl.ANY)
    dma = pltpu.SemaphoreType.DMA
    slots, edge = own.shape[0], own.shape[1]
    tile = (PANEL * edge, SLAB * edge)
    listed = pltpu.VMEM((STEPS,) + ids.shape, ids.dtype)
    return pl.pallas_call(
        functools.partial(product_kernel, stride, bits),
        out_shape=jax.ShapeDtypeStruct(tile, own.dtype),
        in_specs=[any_spec] * 4,
        out_specs=pl.BlockSpec(memory_space=pltpu.VMEM),
        scratch_shapes=[
            pltpu.VMEM((STEPS, 2 * slots, edge, edge), own.dtype),
            pltpu.VMEM((2, STEPS, slab.shape[0] + 1, edge, edge), own.dtype),
            listed, listed, pltpu.VMEM((2, STEPS) + names.shape, names.dtype),
            pltpu.VMEM((2 * slots + 1, edge, edge), own.dtype),
            pltpu.VMEM((PANEL, edge, 2 * SLAB * edge), own.dtype),
            pltpu.VMEM((PANEL * edge, 2 * SLAB * edge), jnp.float32),
            pltpu.VMEM(tile, own.dtype),
            pltpu.VMEM((3 * PANEL, 128), jnp.int32),
            pltpu.SMEM((STEPS, 3 * PANEL, 128), jnp.int32),
            dma((STEPS, CHUNKS + 1)), dma((STEPS, CHUNKS + 1)),
            dma((STEPS, CHUNKS + 1)), dma((STEPS, CHUNKS + 1)), dma((CHUNKS + 1,)),
            dma((2, STEPS, 2)), dma((2, STEPS, 2)), dma((GROUPS,)), dma((GROUPS,)),
            dma((4,)), dma((1,)),
        ],
        compiler_params=pltpu.CompilerParams(
            collective_id=0, has_side_effects=True, vmem_limit_bytes=56 * 2**20
        ),
    )(own, slab, ids, names)


def on_device(stored_blocks, stored_ids, slab_blocks, slab_ids, pair_lists):
    stride = lax.axis_size("col") // STEPS
    bits = lax.axis_size("row").bit_length() - 1
    ids = stored_ids.reshape(stored_ids.shape[2], 1, stored_ids.shape[3])
    names = slab_ids.reshape(slab_ids.shape[2], 1, slab_ids.shape[3])
    return product_call(stored_blocks[0, 0], slab_blocks[0, 0], ids, names, stride, bits)


def solution(mesh):
    return jax.shard_map(
        on_device,
        mesh=mesh,
        in_specs=(
            P("row", "col", None, None, None),
            P("row", "col", None, None),
            P("row", "col", None, None, None),
            P("row", "col", None, None),
            P("row", "col", None, None, None),
        ),
        out_specs=P("row", "col"),
        check_vma=False,
    )
```

time: 157 us -> 161 us (1.025)
  the two profiles are of different devices: /device:TPU:25 before, /device:TPU:27 now
where the time goes in v2:
time: 161 us
  Pallas kernels  159 us (99%)
  local copies, waits for them, and re-layouts  2.26 us (1%)
    pallas_call x1, Pallas kernels, product_call(): pl.pallas_call(functools.partial(product_kernel, stride, bits), out_shape...  159 us

profile of v2, /device:TPU:27, one launch (start us, length us, event | category | flops | bytes accessed | tf_op | source)
XLA Modules:
  0.0 160.9 jit_solution(5522189417461518491)
XLA Ops:
  0.0 158.6 %shard_map.46 = bf16[2048,256]{1,0:T(8,128)(2,1)} custom-call(bf16[64,128,128]{2,1,0:T(8,128)(2,1)} %bitcast.4, bf16[32,128,128]{2,1,0:T(8,128)(2,1)} %bitcast.5, s32[3,1,64]{2,1,0:T(1,128)} %bitcast.6, s32[3,1,32]{2,1,0:T(1,128)} %bitcast.7), custom_call_target="tpu_custom_call" | custom-call | tf_op jit(solution)/shard_map/pallas_call | solution.py:461
  158.6 2.3 %copy.6 = bf16[2048,256]{1,0:T(8,128)(2,1)} copy(bf16[2048,256]{1,0:T(8,128)(2,1)} %shard_map.46) | data formatting | bytes 2097152

commit v3 on v2

--- a/solution.py
+++ b/solution.py
@@ -11,7 +11,7 @@
 SLAB = 2
 STEPS = 4
 CHUNKS = 8
-FORWARDED = 2
+FORWARDED = 1
 GROUPS = 4
 MESH = pl.DeviceIdType.MESH
 
@@ -262,8 +262,11 @@
         fetch.start()
         fetch.wait()
 
+    def lay_slab(s):
+        places = ((0, flipped(s, pos, 2)), (1, flipped(s, fed, 2)))
+
         def slab_row(k, carry):
-            for side, t, _ in places:
+            for side, t in places:
                 for n in range(SLAB):
                     at = side * width + n * edge
                     right_all[k, :, at : at + edge] = slabs[
@@ -276,7 +279,7 @@
         def some(g, carry):
             for x in range(4):
                 block = blocks[s, of + g * 4 + x]
-                stage[1 + to + g * 4 + x] = block.T if turn else block
+                stage[s % 2, 1 + to + g * 4 + x] = block.T if turn else block
             return carry
 
         lax.fori_loop(0, size // 4, some, 0)
@@ -314,11 +317,11 @@
         rows = []
         for a in range(block_rows):
             rows.append(jnp.concatenate(
-                [stage[scalars[s, j, g * block_rows + a]] for j in range(PANEL)], axis=1))
+                [stage[s % 2, scalars[s, j, g * block_rows + a]] for j in range(PANEL)], axis=1))
         return jnp.dot(
             jnp.concatenate(rows, axis=0), right, preferred_element_type=jnp.float32)
 
-    def multiply(s, first):
+    def multiply(s, first, begin, end):
         right = right_all[...].reshape(depth, 2 * width)
 
         def product(g, carry):
@@ -326,16 +329,17 @@
             acc[rows_of(g)] = total if first else total + acc[rows_of(g)]
             return carry
 
-        lax.fori_loop(0, GROUPS, product, 0)
-
-    def take(s, first=False):
+        lax.fori_loop(begin, end, product, 0)
+
+    def tabulate(s):
         crossed(s, 0)
         prepare(s)
-        for ch in range(1, CHUNKS + 1):
+
+    def both(s, *chs):
+        for ch in chs:
             hold_row(s, ch)
             crossed(s, ch)
             hold_pair(s, ch)
-        multiply(s, first)
 
     @pl.when(worker)
     def _():
@@ -356,7 +360,8 @@
         for side in range(2):
             for t in range(STEPS):
                 slabs[side, t, 0] = zero_block
-        stage[0] = zero_block
+        for n in range(2):
+            stage[n, 0] = zero_block
 
         def relay_fed(ch):
             along(landed(fed, ch), fed, ch).wait_recv()
@@ -366,6 +371,9 @@
         for ch in pieces:
             along(landed(near, ch), near, ch).wait_recv()
             send_across(landed(near, ch), near, ch)
+            if ch == 1:
+                for copy in local:
+                    copy.wait()
             if ch == 2:
                 have(0, 2)
                 give(0, 3, plane_one, tiles(0, 2))
@@ -375,6 +383,8 @@
             if ch == 6:
                 for n in range(3):
                     relay_fed(n)
+            if ch >= 2:
+                both(1, ch - 1)
 
         @pl.when(pos == 2)
         def _():
@@ -382,31 +392,76 @@
                 across(landed(pos, ch), pos, ch).wait_recv()
                 forward(ch).start()
 
+        def from_far(ch):
+            along(landed(far, ch), far, ch).wait_recv()
+            send_across(landed(far, ch), far, ch)
+
+        def pairs(s, *chs):
+            for ch in chs:
+                crossed(s, ch)
+                hold_pair(s, ch)
+
+        half = CHUNKS // 2
+        from_far(0)
+        both(1, CHUNKS)
+        for n in range(1, half + 1):
+            hold_row(2, n)
+        from_far(1)
+        for n in range(half + 1, CHUNKS + 1):
+            hold_row(2, n)
         have(1, 2)
         give(1, 3, plane_one, tiles(1, 2))
-        for copy in local:
-            copy.wait()
+        from_far(2)
         have(0, 1)
         have(0, 3)
         have(1, 1)
         have(1, 3)
-
-        take(1, True)
-        for ch in pieces:
-            if ch > 2:
-                relay_fed(ch)
-            along(landed(far, ch), far, ch).wait_recv()
-            send_across(landed(far, ch), far, ch)
-            if ch == 4:
-                take(2)
-        take(0)
+        relay_fed(3)
+        tabulate(1)
+        lay_slab(1)
+        multiply(1, True, 0, 2)
+        relay_fed(4)
+        from_far(3)
+        multiply(1, True, 2, GROUPS)
+        tabulate(2)
+        relay_fed(5)
+        from_far(4)
+        pairs(2, *range(1, CHUNKS + 1))
+        lay_slab(2)
+        relay_fed(6)
+        from_far(5)
+        multiply(2, False, 0, 2)
+        tabulate(0)
+        relay_fed(7)
+        from_far(6)
+        multiply(2, False, 2, GROUPS)
+        tabulate(STEPS - 1)
+        both(0, 1, 2)
+        relay_fed(8)
+
+        @pl.when(pos == 2)
+        def _():
+            from_far(7)
+            from_far(8)
+
+        both(0, *range(3, CHUNKS + 1))
+        both(STEPS - 1, 1, 2)
+
+        @pl.when(pos == 1)
+        def _():
+            from_far(7)
+
+        lay_slab(0)
+        multiply(0, False, 0, 2)
+
+        @pl.when(pos == 1)
+        def _():
+            from_far(8)
+
+        multiply(0, False, 2, GROUPS)
         s = STEPS - 1
-        crossed(s, 0)
-        prepare(s)
-        for ch in range(1, CHUNKS + 1):
-            hold_row(s, ch)
-            crossed(s, ch)
-            hold_pair(s, ch)
+        lay_slab(s)
+        both(s, *range(3, CHUNKS + 1))
         right = right_all[:, :, width:].reshape(depth, width)
 
         def last_away(g, carry):
@@ -467,7 +522,7 @@
             pltpu.VMEM((STEPS, 2 * slots, edge, edge), own.dtype),
             pltpu.VMEM((2, STEPS, slab.shape[0] + 1, edge, edge), own.dtype),
             listed, listed, pltpu.VMEM((2, STEPS) + names.shape, names.dtype),
-            pltpu.VMEM((2 * slots + 1, edge, edge), own.dtype),
+            pltpu.VMEM((2, 2 * slots + 1, edge, edge), own.dtype),
             pltpu.VMEM((PANEL, edge, 2 * SLAB * edge), own.dtype),
             pltpu.VMEM((PANEL * edge, 2 * SLAB * edge), jnp.float32),
             pltpu.VMEM(tile, own.dtype),

time: 161 us -> 143 us (0.89)
  the two profiles are of different devices: /device:TPU:27 before, /device:TPU:25 now
where the time goes in v3:
time: 143 us; the launch traced here: 140 us
  Pallas kernels  138 us (97%)
  local copies, waits for them, and re-layouts  2.26 us (2%)
    pallas_call x1, Pallas kernels, product_call(): pl.pallas_call(functools.partial(product_kernel, stride, bits), out_shape...  138 us

profile of v3, /device:TPU:25, one launch (start us, length us, event | category | flops | bytes accessed | tf_op | source)
XLA Modules:
  0.0 140.5 jit_solution(13212925711246552905)
XLA Ops:
  0.0 138.2 %shard_map.46 = bf16[2048,256]{1,0:T(8,128)(2,1)} custom-call(bf16[64,128,128]{2,1,0:T(8,128)(2,1)} %bitcast.4, bf16[32,128,128]{2,1,0:T(8,128)(2,1)} %bitcast.5, s32[3,1,64]{2,1,0:T(1,128)} %bitcast.6, s32[3,1,32]{2,1,0:T(1,128)} %bitcast.7), custom_call_target="tpu_custom_call" | custom-call | tf_op jit(solution)/shard_map/pallas_call | solution.py:516
  138.2 2.3 %copy.6 = bf16[2048,256]{1,0:T(8,128)(2,1)} copy(bf16[2048,256]{1,0:T(8,128)(2,1)} %shard_map.46) | data formatting | bytes 2097152

commit v4 on v3

--- a/solution.py
+++ b/solution.py
@@ -12,6 +12,7 @@
 STEPS = 4
 CHUNKS = 8
 FORWARDED = 1
+PUT_OFF = 4
 GROUPS = 4
 MESH = pl.DeviceIdType.MESH
 
@@ -201,10 +202,29 @@
     def held_back(s, ch):
         return s == pos + 1 if ch in tail else False
 
+    second_core = partner(STEPS - 1) % 2 == 1
+    late = range(CHUNKS + 1 - PUT_OFF, CHUNKS + 1)
+
+    def waits_longer(ch):
+        if ch == late[0]:
+            return jnp.logical_and(second_core, pos == 2)
+        return second_core
+
     def send_across(src, s, ch):
-        @pl.when(jnp.logical_and(cond_kind(s), jnp.logical_not(held_back(s, ch))))
+        sends = jnp.logical_and(cond_kind(s), jnp.logical_not(held_back(s, ch)))
+        if ch in late:
+            put_off = jnp.logical_and(s == STEPS - 1, waits_longer(ch))
+            sends = jnp.logical_and(sends, jnp.logical_not(put_off))
+
+        @pl.when(sends)
         def _():
             across(src, s, ch).start()
+
+    def send_late():
+        for ch in late:
+            @pl.when(jnp.logical_and(waits_longer(ch), jnp.logical_not(held_back(STEPS - 1, ch))))
+            def _():
+                across(landed(STEPS - 1, ch), STEPS - 1, ch).start()
 
     def crossed(s, ch):
         waits = cond_kind(s)
@@ -269,7 +289,7 @@
             for side, t in places:
                 for n in range(SLAB):
                     at = side * width + n * edge
-                    right_all[k, :, at : at + edge] = slabs[
+                    right_all[s // 2, k, :, at : at + edge] = slabs[
                         side, t, scalars[s, (1 + side) * PANEL + k, n]]
             return carry
 
@@ -279,7 +299,7 @@
         def some(g, carry):
             for x in range(4):
                 block = blocks[s, of + g * 4 + x]
-                stage[s % 2, 1 + to + g * 4 + x] = block.T if turn else block
+                stage[s // 2, 1 + to + g * 4 + x] = block.T if turn else block
             return carry
 
         lax.fori_loop(0, size // 4, some, 0)
@@ -317,12 +337,12 @@
         rows = []
         for a in range(block_rows):
             rows.append(jnp.concatenate(
-                [stage[s % 2, scalars[s, j, g * block_rows + a]] for j in range(PANEL)], axis=1))
+                [stage[s // 2, scalars[s, j, g * block_rows + a]] for j in range(PANEL)], axis=1))
         return jnp.dot(
             jnp.concatenate(rows, axis=0), right, preferred_element_type=jnp.float32)
 
     def multiply(s, first, begin, end):
-        right = right_all[...].reshape(depth, 2 * width)
+        right = right_all[s // 2].reshape(depth, 2 * width)
 
         def product(g, carry):
             total = some_rows(s, g, right)
@@ -428,44 +448,58 @@
         from_far(4)
         pairs(2, *range(1, CHUNKS + 1))
         lay_slab(2)
+        both(0, 1, 2)
         relay_fed(6)
         from_far(5)
         multiply(2, False, 0, 2)
         tabulate(0)
+        both(0, 3)
         relay_fed(7)
         from_far(6)
         multiply(2, False, 2, GROUPS)
         tabulate(STEPS - 1)
-        both(0, 1, 2)
+        both(0, 4)
         relay_fed(8)
 
         @pl.when(pos == 2)
         def _():
-            from_far(7)
+            send_late()
+
+        lay_slab(0)
+        lay_slab(STEPS - 1)
+        both(0, 5, 6)
+        from_far(7)
+        both(0, 7)
+        both(STEPS - 1, 1, 2)
+        for n in range(3, 7):
+            hold_row(STEPS - 1, n)
+
+        @pl.when(pos == 2)
+        def _():
             from_far(8)
 
-        both(0, *range(3, CHUNKS + 1))
-        both(STEPS - 1, 1, 2)
+        both(0, 8)
+
+        def away(s):
+            return right_all[s // 2][:, :, width:].reshape(depth, width)
+
+        def first_away(g, carry):
+            acc[rows_of(g), width:] += some_rows(0, g, away(0))
+            return carry
+
+        lax.fori_loop(0, GROUPS, first_away, 0)
 
         @pl.when(pos == 1)
         def _():
-            from_far(7)
-
-        lay_slab(0)
-        multiply(0, False, 0, 2)
-
-        @pl.when(pos == 1)
-        def _():
             from_far(8)
-
-        multiply(0, False, 2, GROUPS)
+            send_late()
+
         s = STEPS - 1
-        lay_slab(s)
-        both(s, *range(3, CHUNKS + 1))
-        right = right_all[:, :, width:].reshape(depth, width)
+        pairs(s, *range(3, 7))
+        both(s, 7, 8)
 
         def last_away(g, carry):
-            total = some_rows(s, g, right) + acc[rows_of(g), width:]
+            total = some_rows(s, g, away(s)) + acc[rows_of(g), width:]
             result[rows_of(g)] = total.astype(result.dtype)
 
             @pl.when(g > 0)
@@ -474,10 +508,13 @@
             return carry
 
         lax.fori_loop(0, GROUPS, last_away, 0)
-        kept = right_all[:, :, :width].reshape(depth, width)
+
+        def here(s):
+            return right_all[s // 2][:, :, :width].reshape(depth, width)
 
         def last_here(g, carry):
-            total = some_rows(s, g, kept) + acc[rows_of(g), :width]
+            total = some_rows(s, g, here(s)) + acc[rows_of(g), :width]
+            total = total + some_rows(0, g, here(0))
             out[rows_of(g)] = total.astype(out.dtype)
 
             @pl.when(g == 0)
@@ -523,7 +560,7 @@
             pltpu.VMEM((2, STEPS, slab.shape[0] + 1, edge, edge), own.dtype),
             listed, listed, pltpu.VMEM((2, STEPS) + names.shape, names.dtype),
             pltpu.VMEM((2, 2 * slots + 1, edge, edge), own.dtype),
-            pltpu.VMEM((PANEL, edge, 2 * SLAB * edge), own.dtype),
+            pltpu.VMEM((2, PANEL, edge, 2 * SLAB * edge), own.dtype),
             pltpu.VMEM((PANEL * edge, 2 * SLAB * edge), jnp.float32),
             pltpu.VMEM(tile, own.dtype),
             pltpu.VMEM((3 * PANEL, 128), jnp.int32),

time: 143 us -> 138 us (0.965); the launches traced: 140 us -> 138 us
  Pallas kernels: 138 us -> 136 us
    pallas_call x1, Pallas kernels: 138 us -> 136 us  [product_call(): pl.pallas_call(functools.partial(product_kernel, stride, bits), out_shape...]
where the time goes in v4:
time: 138 us
  Pallas kernels  136 us (99%)
  local copies, waits for them, and re-layouts  2.26 us (2%)
    pallas_call x1, Pallas kernels, product_call(): pl.pallas_call(functools.partial(product_kernel, stride, bits), out_shape...  136 us

profile of v4, /device:TPU:25, one launch (start us, length us, event | category | flops | bytes accessed | tf_op | source)
XLA Modules:
  0.0 138.3 jit_solution(845359598859259216)
XLA Ops:
  0.0 136.0 %shard_map.46 = bf16[2048,256]{1,0:T(8,128)(2,1)} custom-call(bf16[64,128,128]{2,1,0:T(8,128)(2,1)} %bitcast.4, bf16[32,128,128]{2,1,0:T(8,128)(2,1)} %bitcast.5, s32[3,1,64]{2,1,0:T(1,128)} %bitcast.6, s32[3,1,32]{2,1,0:T(1,128)} %bitcast.7), custom_call_target="tpu_custom_call" | custom-call | tf_op jit(solution)/shard_map/pallas_call | solution.py:553
  136.0 2.3 %copy.6 = bf16[2048,256]{1,0:T(8,128)(2,1)} copy(bf16[2048,256]{1,0:T(8,128)(2,1)} %shard_map.46) | data formatting | bytes 2097152
